TPU v7x, 32 devices: a whole 2x2x4 slice. The times are simulated.
32 devices in a mesh: grp: 2 (over y), cell: 4 (over z), snap: 2 (over x), var: 2 (over core).
Axes of the slice: x: 2, y: 2, z: 4, core: 2. Of those that a mesh axis runs over, the one named last changes fastest.
Arguments:
- q_true: bfloat16 [64, 10, 2048], P(('snap', 'var'), 'grp', 'cell'), parts along dimension 1, may hold values from -6 to 6
- coeffs: bfloat16 [64, 256], P(('snap', 'var'), 'grp'), parts along dimension 1, may hold values from -0.5 to 0.5
- basis: bfloat16 [128, 10, 2048], P(('snap', 'var'), 'grp', 'cell'), parts along dimension 1, may hold values from -6 to 6
- weights: float32 [10, 2048], P('grp', 'cell'), parts along dimension 0, may hold values from 0.0029646354 to 0.029646354
- geometry: float32 [12, 2048], P('grp', 'cell'), parts along dimension 0, may hold values from 0.2 to 1
- neighbors: int32 [12, 2048], P('grp', 'cell'), parts along dimension 0, may hold values from 0 to 767, as said below
- send_rows: int32 [4, 4, 128], P('cell', 'grp'), parts along dimension 1, may hold values from 0 to 511, as said below
- block_count: int32 [4, 2], P('cell', 'grp'), parts along dimension 1, may hold values from 2 to 4
Outputs:
- closure: float32 [64, 256], P(('snap', 'var'), 'grp'), parts along dimension 1
There are 2 independent parts, one for each index of `grp`. A program takes and returns all parts, laid end to end along the dimension named above; each array names one. Nothing has to cross between parts.
Inputs may be any that keep to these rules, and one draw needn't show every extreme that they name: neighbors[k, c] indexes a list made of the 512 cells of c's own cell shard, then the 128 cells received from the shard before, then the 128 cells received from the shard after. `send_rows`: indices local to the sending cell shard.
All inputs are finite; a program needn't handle non-finite values.
Results may differ from a plain program's by a relative error of at most 0.00091.
Values may be sent and summed in bfloat16 or wider, within the bound.
A program may use at most 64 MiB of HBM per device.

v0:
```python
import math
import jax
import jax.numpy as jnp
from jax import lax
from jax.sharding import PartitionSpec as P

BLOCK = 128


def from_behind(shard, axis, by):
    peers = lax.axis_size(axis)
    pairs = [(i, i + by) for i in range(peers) if 0 <= i + by < peers]
    return lax.ppermute(shard, axis, pairs)


def face_flux(extended, geometry, neighbors):
    cell_count = geometry.shape[1]
    var_count = extended.shape[1]
    own_cells = extended[:, :, :cell_count]
    product = extended * extended[:, 1:2, :]
    own_product = product[:, :, :cell_count]
    stacked = jnp.concatenate([extended, product], axis=1)
    running = jnp.zeros(own_cells.shape, jnp.float32)
    for face_index in range(geometry.shape[0]):
        taken = jnp.take(stacked, neighbors[face_index], axis=2)
        beside = taken[:, :var_count]
        beside_product = taken[:, var_count:]
        running = running + geometry[face_index] * (
            0.5 * (own_product + beside_product) - 0.5 * (beside - own_cells)
        )
    return running


def local(q_true, coeffs, basis, weights, geometry, neighbors, send_rows, block_count):
    snap_count, var_count, cell_count = q_true.shape
    send_lists = send_rows[0]

    def rim_rows(field):
        return (jnp.take(field, send_lists[0], axis=2), jnp.take(field, send_lists[1], axis=2))

    true_to_prev, true_to_next = rim_rows(q_true)
    whole_basis = lax.all_gather(basis, ("snap", "var"), axis=0, tiled=True)
    basis_flat = whole_basis.reshape(whole_basis.shape[0], var_count * cell_count)
    rebuilt_sum = jnp.dot(coeffs, basis_flat, preferred_element_type=jnp.float32)
    rebuilt = rebuilt_sum.astype(jnp.bfloat16).reshape(snap_count, var_count, cell_count)
    rebuilt_to_prev, rebuilt_to_next = rim_rows(rebuilt)
    true_from_prev = from_behind(true_to_next, "cell", 1)
    true_from_next = from_behind(true_to_prev, "cell", -1)
    rebuilt_from_prev = from_behind(rebuilt_to_next, "cell", 1)
    rebuilt_from_next = from_behind(rebuilt_to_prev, "cell", -1)
    true_ext = jnp.concatenate([q_true, true_from_prev, true_from_next], axis=2)
    rebuilt_ext = jnp.concatenate([rebuilt, rebuilt_from_prev, rebuilt_from_next], axis=2)
    positions = jnp.arange(cell_count, dtype=jnp.int32)
    live = (positions < block_count[0, 0] * BLOCK).astype(jnp.float32)
    group = math.gcd(snap_count, 8)
    ext_count = true_ext.shape[2]

    def snap_block(pair):
        true_part, rebuilt_part = pair
        flux_true = face_flux(true_part.astype(jnp.float32), geometry, neighbors)
        flux_rebuilt = face_flux(rebuilt_part.astype(jnp.float32), geometry, neighbors)
        return (weights * live * (flux_true - flux_rebuilt)).astype(jnp.bfloat16)

    true_groups = true_ext.reshape(snap_count // group, group, var_count, ext_count)
    rebuilt_groups = rebuilt_ext.reshape(snap_count // group, group, var_count, ext_count)
    weighted = lax.map(snap_block, (true_groups, rebuilt_groups))
    weighted_flat = weighted.reshape(snap_count, var_count * cell_count)
    contract = (((1,), (1,)), ((), ()))
    closure_part = lax.dot_general(
        weighted_flat, basis_flat, contract, preferred_element_type=jnp.float32
    )
    return lax.psum(closure_part, "cell")


def solution(mesh):
    in_specs = (
        P(("snap", "var"), "grp", "cell"),
        P(("snap", "var"), "grp"),
        P(("snap", "var"), "grp", "cell"),
        P("grp", "cell"),
        P("grp", "cell"),
        P("grp", "cell"),
        P("cell", "grp", None),
        P("cell", "grp"),
    )
    out_specs = P(("snap", "var"), "grp")
    return jax.shard_map(local, mesh=mesh, in_specs=in_specs, out_specs=out_specs, check_vma=False)
```

profile of v0, /device:TPU:0, one launch (start us, length us, event | category | flops | bytes accessed | tf_op | source)
XLA Modules:
  0.0 230.5 jit_solution(12883758674813576312)
XLA Ops:
  0.8 9.7 %all_gather.3 = bf16[128,5,512]{2,0,1:T(8,128)(2,1)S(1)} all-gather(bf16[32,5,512]{2,0,1:T(8,128)(2,1)} %param.16), channel_id=1, replica_groups=mesh['grp'=2,'cell'=4,'snap'=2,'var'=2] {'snap','var'}, dimensions={0}, use_global_device_ids=true | all-gather | bytes 819200 | tf_op jit(solution)/shard_map/all_gather | solution.py:42
  15.2 3.5 %collective-permute-start = (bf16[16,5,128]{0,1,2:T(8,128)(2,1)}, bf16[16,5,128]{0,1,2:T(8,128)(2,1)S(1)}, u32[]{:S(2)}, u32[]{:S(2)}) collective-permute-start(bf16[16,5,128]{0,1,2:T(8,128)(2,1)} %get-tuple-element.158), channel_id=1, source_target_pairs={{0,4},{4,8},{8,12},{1,5},{5,9},{9,13},{2,6},{6,10},{10,14},{3,7},{... | collective-permute-start | bytes 61448 | tf_op jit(solution)/shard_map/ppermute | solution.py:13
  21.6 4.6 %collective-permute-start.2 = (bf16[16,5,128]{0,1,2:T(8,128)(2,1)}, bf16[16,5,128]{0,1,2:T(8,128)(2,1)S(1)}, u32[]{:S(2)}, u32[]{:S(2)}) collective-permute-start(bf16[16,5,128]{0,1,2:T(8,128)(2,1)} %get-tuple-element.157), channel_id=1, source_target_pairs={{0,4},{4,8},{8,12},{1,5},{5,9},{9,13},{2,6},{6,10},{10,14},{3,7},{... | collective-permute-start | bytes 61448 | tf_op jit(solution)/shard_map/ppermute | solution.py:13
  32.1 4.0 %collective-permute-done.3 = bf16[16,5,128]{0,1,2:T(8,128)(2,1)S(1)} collective-permute-done((bf16[16,5,128]{0,1,2:T(8,128)(2,1)S(1)}, bf16[16,5,128]{0,1,2:T(8,128)(2,1)S(1)}, u32[]{:S(2)}, u32[]{:S(2)}) %collective-permute-start.3) | collective-permute-done | bytes 20512 | tf_op jit(solution)/shard_map/ppermute | solution.py:13
  36.9 181.6 %while.11 = (s32[]{:T(128)}, bf16[2,8,5,512]{3,1,2,0:T(8,128)(2,1)}, f32[5,512]{1,0:T(8,128)S(1)}, f32[6,512]{1,0:T(8,128)}, bf16[2,8,5,768]{3,1,0,2:T(8,128)(2,...) while((s32[]{:T(128)}, ...), condition=%wide.region_1.4_spmd.clone, body=%wide.region_0.3_spmd.clone.sunk | while | flops 2576898 | bytes 26133308 | solution.py:66
  49.7 2.8 %gather_fusion.11 = f32[512,8,10]{2,1,0:T(8,128)} fusion(f32[8,10,768]{1,0,2:T(8,128)S(1)} %copy.153, s32[1024]{0:T(1024)} %pad_clamp_fusion.19), kind=kCustom, calls=%fused_computation.10.clone.clone.1 | custom fusion | bytes 329728 | tf_op jit(solution)/shard_map/while/body/eval_jaxpr/jit(_take)/gather | solution.py:25
  52.5 2.9 %copy.164 = f32[512,8,10]{0,1,2:T(8,128)} copy(f32[512,8,10]{2,1,0:T(8,128)} %gather_fusion.11) | data formatting | bytes 327680 | tf_op jit(solution)/shard_map/while/body/eval_jaxpr/jit(_take)/gather | solution.py:25
  58.1 2.9 %copy.162 = f32[512,8,10]{0,1,2:T(8,128)} copy(f32[512,8,10]{2,1,0:T(8,128)} %gather_fusion.9) | data formatting | bytes 327680 | tf_op jit(solution)/shard_map/while/body/eval_jaxpr/jit(_take)/gather | solution.py:25
  63.6 2.9 %copy.160 = f32[512,8,10]{0,1,2:T(8,128)} copy(f32[512,8,10]{2,1,0:T(8,128)} %gather_fusion.7) | data formatting | bytes 327680 | tf_op jit(solution)/shard_map/while/body/eval_jaxpr/jit(_take)/gather | solution.py:25
  69.2 2.9 %copy.158 = f32[512,8,10]{0,1,2:T(8,128)} copy(f32[512,8,10]{2,1,0:T(8,128)} %gather_fusion.5) | data formatting | bytes 327680 | tf_op jit(solution)/shard_map/while/body/eval_jaxpr/jit(_take)/gather | solution.py:25
  74.8 2.9 %copy.156 = f32[512,8,10]{0,1,2:T(8,128)} copy(f32[512,8,10]{2,1,0:T(8,128)} %gather_fusion.3) | data formatting | bytes 327680 | tf_op jit(solution)/shard_map/while/body/eval_jaxpr/jit(_take)/gather | solution.py:25
  80.3 2.9 %copy.154 = f32[512,8,10]{0,1,2:T(8,128)} copy(f32[512,8,10]{2,1,0:T(8,128)} %gather_fusion.1) | data formatting | bytes 327680 | tf_op jit(solution)/shard_map/while/body/eval_jaxpr/jit(_take)/gather | solution.py:25
  85.4 2.8 %gather_fusion.10 = f32[512,8,10]{2,1,0:T(8,128)} fusion(f32[8,10,768]{1,0,2:T(8,128)S(1)} %copy.151, s32[1024]{0:T(1024)} %pad_clamp_fusion.19), kind=kCustom, calls=%fused_computation.1.clone.clone.1 | custom fusion | bytes 329728 | tf_op jit(solution)/shard_map/while/body/eval_jaxpr/jit(_take)/gather | solution.py:25
  88.2 2.9 %copy.163 = f32[512,8,10]{0,1,2:T(8,128)} copy(f32[512,8,10]{2,1,0:T(8,128)} %gather_fusion.10) | data formatting | bytes 327680 | tf_op jit(solution)/shard_map/while/body/eval_jaxpr/jit(_take)/gather | solution.py:25
  95.5 2.9 %copy.161 = f32[512,8,10]{0,1,2:T(8,128)} copy(f32[512,8,10]{2,1,0:T(8,128)} %gather_fusion.8) | data formatting | bytes 327680 | tf_op jit(solution)/shard_map/while/body/eval_jaxpr/jit(_take)/gather | solution.py:25
  102.9 2.9 %copy.159 = f32[512,8,10]{0,1,2:T(8,128)} copy(f32[512,8,10]{2,1,0:T(8,128)} %gather_fusion.6) | data formatting | bytes 327680 | tf_op jit(solution)/shard_map/while/body/eval_jaxpr/jit(_take)/gather | solution.py:25
  110.3 2.9 %copy.157 = f32[512,8,10]{0,1,2:T(8,128)} copy(f32[512,8,10]{2,1,0:T(8,128)} %gather_fusion.4) | data formatting | bytes 327680 | tf_op jit(solution)/shard_map/while/body/eval_jaxpr/jit(_take)/gather | solution.py:25
  117.6 2.9 %copy.155 = f32[512,8,10]{0,1,2:T(8,128)} copy(f32[512,8,10]{2,1,0:T(8,128)} %gather_fusion.2) | data formatting | bytes 327680 | tf_op jit(solution)/shard_map/while/body/eval_jaxpr/jit(_take)/gather | solution.py:25
  140.5 2.8 %gather_fusion.11 = f32[512,8,10]{2,1,0:T(8,128)} fusion(f32[8,10,768]{1,0,2:T(8,128)S(1)} %copy.153, s32[1024]{0:T(1024)} %pad_clamp_fusion.19), kind=kCustom, calls=%fused_computation.10.clone.clone.1 | custom fusion | bytes 329728 | tf_op jit(solution)/shard_map/while/body/eval_jaxpr/jit(_take)/gather | solution.py:25
  143.3 2.9 %copy.164 = f32[512,8,10]{0,1,2:T(8,128)} copy(f32[512,8,10]{2,1,0:T(8,128)} %gather_fusion.11) | data formatting | bytes 327680 | tf_op jit(solution)/shard_map/while/body/eval_jaxpr/jit(_take)/gather | solution.py:25
  148.9 2.9 %copy.162 = f32[512,8,10]{0,1,2:T(8,128)} copy(f32[512,8,10]{2,1,0:T(8,128)} %gather_fusion.9) | data formatting | bytes 327680 | tf_op jit(solution)/shard_map/while/body/eval_jaxpr/jit(_take)/gather | solution.py:25
  154.4 2.9 %copy.160 = f32[512,8,10]{0,1,2:T(8,128)} copy(f32[512,8,10]{2,1,0:T(8,128)} %gather_fusion.7) | data formatting | bytes 327680 | tf_op jit(solution)/shard_map/while/body/eval_jaxpr/jit(_take)/gather | solution.py:25
  160.0 2.9 %copy.158 = f32[512,8,10]{0,1,2:T(8,128)} copy(f32[512,8,10]{2,1,0:T(8,128)} %gather_fusion.5) | data formatting | bytes 327680 | tf_op jit(solution)/shard_map/while/body/eval_jaxpr/jit(_take)/gather | solution.py:25
  165.6 2.9 %copy.156 = f32[512,8,10]{0,1,2:T(8,128)} copy(f32[512,8,10]{2,1,0:T(8,128)} %gather_fusion.3) | data formatting | bytes 327680 | tf_op jit(solution)/shard_map/while/body/eval_jaxpr/jit(_take)/gather | solution.py:25
  171.1 2.9 %copy.154 = f32[512,8,10]{0,1,2:T(8,128)} copy(f32[512,8,10]{2,1,0:T(8,128)} %gather_fusion.1) | data formatting | bytes 327680 | tf_op jit(solution)/shard_map/while/body/eval_jaxpr/jit(_take)/gather | solution.py:25
  176.2 2.8 %gather_fusion.10 = f32[512,8,10]{2,1,0:T(8,128)} fusion(f32[8,10,768]{1,0,2:T(8,128)S(1)} %copy.151, s32[1024]{0:T(1024)} %pad_clamp_fusion.19), kind=kCustom, calls=%fused_computation.1.clone.clone.1 | custom fusion | bytes 329728 | tf_op jit(solution)/shard_map/while/body/eval_jaxpr/jit(_take)/gather | solution.py:25
  179.0 2.9 %copy.163 = f32[512,8,10]{0,1,2:T(8,128)} copy(f32[512,8,10]{2,1,0:T(8,128)} %gather_fusion.10) | data formatting | bytes 327680 | tf_op jit(solution)/shard_map/while/body/eval_jaxpr/jit(_take)/gather | solution.py:25
  186.3 2.9 %copy.161 = f32[512,8,10]{0,1,2:T(8,128)} copy(f32[512,8,10]{2,1,0:T(8,128)} %gather_fusion.8) | data formatting | bytes 327680 | tf_op jit(solution)/shard_map/while/body/eval_jaxpr/jit(_take)/gather | solution.py:25
  193.7 2.9 %copy.159 = f32[512,8,10]{0,1,2:T(8,128)} copy(f32[512,8,10]{2,1,0:T(8,128)} %gather_fusion.6) | data formatting | bytes 327680 | tf_op jit(solution)/shard_map/while/body/eval_jaxpr/jit(_take)/gather | solution.py:25
  201.1 2.9 %copy.157 = f32[512,8,10]{0,1,2:T(8,128)} copy(f32[512,8,10]{2,1,0:T(8,128)} %gather_fusion.4) | data formatting | bytes 327680 | tf_op jit(solution)/shard_map/while/body/eval_jaxpr/jit(_take)/gather | solution.py:25
  208.4 2.9 %copy.155 = f32[512,8,10]{0,1,2:T(8,128)} copy(f32[512,8,10]{2,1,0:T(8,128)} %gather_fusion.2) | data formatting | bytes 327680 | tf_op jit(solution)/shard_map/while/body/eval_jaxpr/jit(_take)/gather | solution.py:25
  219.8 10.7 %psum.7 = f32[16,128]{1,0:T(8,128)} all-reduce(f32[16,128]{1,0:T(8,128)S(1)} %fusion.66), channel_id=1, replica_groups=mesh['grp'=2,'cell'=4,'snap'=2,'var'=2] {'cell'}, use_global_device_ids=true, to_apply=%region_2.5 | all-reduce | flops 2048 | bytes 16384 | tf_op jit(solution)/shard_map/psum | solution.py:72
  (233 shorter events, 121.8 us)
Async XLA Ops:
  0.0 10.8 %copy-start = (bf16[16,128]{1,0:T(8,128)(2,1)S(1)}, bf16[16,128]{1,0:T(8,128)(2,1)}, u32[]{:S(2)}) copy-start(bf16[16,128]{1,0:T(8,128)(2,1)} %param.15) | copy-start | bytes 12292
  0.8 11.3 %copy-start.17 = (bf16[16,5,512]{2,0,1:T(8,128)(2,1)S(1)}, bf16[16,5,512]{2,0,1:T(8,128)(2,1)}, u32[]{:S(2)}) copy-start(bf16[16,5,512]{2,0,1:T(8,128)(2,1)} %param.14) | copy-start | bytes 245764
  10.8 4.4 %copy-start.14 = (bf16[128,5,512]{0,2,1:T(8,128)(2,1)}, bf16[128,5,512]{0,2,1:T(8,128)(2,1)S(1)}, u32[]{:S(2)}) copy-start(bf16[128,5,512]{0,2,1:T(8,128)(2,1)S(1)} %copy.124) | copy-start | bytes 1966084
  12.8 24.1 %copy-start.15 = (f32[5,512]{1,0:T(8,128)S(1)}, f32[5,512]{1,0:T(8,128)}, u32[]{:S(2)}) copy-start(f32[5,512]{1,0:T(8,128)} %param.17) | copy-start | bytes 30724
  15.2 12.9 %collective-permute-start = (bf16[16,5,128]{0,1,2:T(8,128)(2,1)}, bf16[16,5,128]{0,1,2:T(8,128)(2,1)S(1)}, u32[]{:S(2)}, u32[]{:S(2)}) collective-permute-start(bf16[16,5,128]{0,1,2:T(8,128)(2,1)} %get-tuple-element.158), channel_id=1, source_target_pairs={{0,4},{4,8},{8,12},{1,5},{5,9},{9,13},{2,6},{6,10},{10,14},{3,7},{... | collective-permute-start | bytes 61448 | tf_op jit(solution)/shard_map/ppermute | solution.py:13
  20.3 10.4 %collective-permute-start.1 = (bf16[16,5,128]{0,1,2:T(8,128)(2,1)S(1)}, bf16[16,5,128]{0,1,2:T(8,128)(2,1)S(1)}, u32[]{:S(2)}, u32[]{:S(2)}) collective-permute-start(bf16[16,5,128]{0,1,2:T(8,128)(2,1)S(1)} %get-tuple-element.160), channel_id=1, source_target_pairs={{4,0},{8,4},{12,8},{5,1},{9,5},{13,9},{6,2},{10,6},{14,10},{7,3},{... | collective-permute-start | bytes 61448 | tf_op jit(solution)/shard_map/ppermute | solution.py:13
  21.6 10.4 %collective-permute-start.2 = (bf16[16,5,128]{0,1,2:T(8,128)(2,1)}, bf16[16,5,128]{0,1,2:T(8,128)(2,1)S(1)}, u32[]{:S(2)}, u32[]{:S(2)}) collective-permute-start(bf16[16,5,128]{0,1,2:T(8,128)(2,1)} %get-tuple-element.157), channel_id=1, source_target_pairs={{0,4},{4,8},{8,12},{1,5},{5,9},{9,13},{2,6},{6,10},{10,14},{3,7},{... | collective-permute-start | bytes 61448 | tf_op jit(solution)/shard_map/ppermute | solution.py:13
  26.2 9.9 %collective-permute-start.3 = (bf16[16,5,128]{0,1,2:T(8,128)(2,1)S(1)}, bf16[16,5,128]{0,1,2:T(8,128)(2,1)S(1)}, u32[]{:S(2)}, u32[]{:S(2)}) collective-permute-start(bf16[16,5,128]{0,1,2:T(8,128)(2,1)S(1)} %get-tuple-element.159), channel_id=1, source_target_pairs={{4,0},{8,4},{12,8},{5,1},{9,5},{13,9},{6,2},{10,6},{14,10},{7,3},{... | collective-permute-start | bytes 61448 | tf_op jit(solution)/shard_map/ppermute | solution.py:13
  98.4 7.4 %copy-start.28 = (pred[512]{0:T(512)(128)(4,1)S(1)}, pred[512]{0:T(512)(128)(4,1)}, u32[]{:S(2)}) copy-start(pred[512]{0:T(512)(128)(4,1)} %compare_and_fusion.17) | copy-start | bytes 1540 | tf_op jit(solution)/shard_map/while
  105.8 7.4 %copy-start.27 = (pred[512]{0:T(512)(128)(4,1)S(1)}, pred[512]{0:T(512)(128)(4,1)}, u32[]{:S(2)}) copy-start(pred[512]{0:T(512)(128)(4,1)} %compare_and_fusion.16) | copy-start | bytes 1540 | tf_op jit(solution)/shard_map/while
  120.5 6.1 %copy-start.18 = (f32[1,512]{1,0:T(1,128)S(1)}, f32[1,512]{1,0:T(1,128)}, u32[]{:S(2)}) copy-start(f32[1,512]{1,0:T(1,128)} %get-tuple-element.261) | copy-start | bytes 6148 | tf_op jit(solution)/shard_map/while
  120.5 6.1 %copy-start.19 = (f32[1,512]{1,0:T(1,128)S(1)}, f32[1,512]{1,0:T(1,128)}, u32[]{:S(2)}) copy-start(f32[1,512]{1,0:T(1,128)} %get-tuple-element.251) | copy-start | bytes 6148 | tf_op jit(solution)/shard_map/while
  120.5 6.1 %copy-start.20 = (f32[1,512]{1,0:T(1,128)S(1)}, f32[1,512]{1,0:T(1,128)}, u32[]{:S(2)}) copy-start(f32[1,512]{1,0:T(1,128)} %get-tuple-element.253) | copy-start | bytes 6148 | tf_op jit(solution)/shard_map/while
  120.5 6.1 %copy-start.21 = (f32[1,512]{1,0:T(1,128)S(1)}, f32[1,512]{1,0:T(1,128)}, u32[]{:S(2)}) copy-start(f32[1,512]{1,0:T(1,128)} %get-tuple-element.255) | copy-start | bytes 6148 | tf_op jit(solution)/shard_map/while
  189.2 7.4 %copy-start.28 = (pred[512]{0:T(512)(128)(4,1)S(1)}, pred[512]{0:T(512)(128)(4,1)}, u32[]{:S(2)}) copy-start(pred[512]{0:T(512)(128)(4,1)} %compare_and_fusion.17) | copy-start | bytes 1540 | tf_op jit(solution)/shard_map/while
  196.6 7.4 %copy-start.27 = (pred[512]{0:T(512)(128)(4,1)S(1)}, pred[512]{0:T(512)(128)(4,1)}, u32[]{:S(2)}) copy-start(pred[512]{0:T(512)(128)(4,1)} %compare_and_fusion.16) | copy-start | bytes 1540 | tf_op jit(solution)/shard_map/while
  211.3 6.1 %copy-start.18 = (f32[1,512]{1,0:T(1,128)S(1)}, f32[1,512]{1,0:T(1,128)}, u32[]{:S(2)}) copy-start(f32[1,512]{1,0:T(1,128)} %get-tuple-element.261) | copy-start | bytes 6148 | tf_op jit(solution)/shard_map/while
  211.3 6.1 %copy-start.19 = (f32[1,512]{1,0:T(1,128)S(1)}, f32[1,512]{1,0:T(1,128)}, u32[]{:S(2)}) copy-start(f32[1,512]{1,0:T(1,128)} %get-tuple-element.251) | copy-start | bytes 6148 | tf_op jit(solution)/shard_map/while
  211.3 6.1 %copy-start.20 = (f32[1,512]{1,0:T(1,128)S(1)}, f32[1,512]{1,0:T(1,128)}, u32[]{:S(2)}) copy-start(f32[1,512]{1,0:T(1,128)} %get-tuple-element.253) | copy-start | bytes 6148 | tf_op jit(solution)/shard_map/while
  211.3 6.1 %copy-start.21 = (f32[1,512]{1,0:T(1,128)S(1)}, f32[1,512]{1,0:T(1,128)}, u32[]{:S(2)}) copy-start(f32[1,512]{1,0:T(1,128)} %get-tuple-element.255) | copy-start | bytes 6148 | tf_op jit(solution)/shard_map/while
  214.0 3.4 %copy-start.2 = (f32[8,5,768]{2,0,1:T(8,128)S(1)}, f32[8,5,768]{2,0,1:T(8,128)}, u32[]{:S(2)}) copy-start(f32[8,5,768]{2,0,1:T(8,128)} %copy-done.1) | copy-start | bytes 368644 | tf_op jit(solution)/shard_map/while
  214.0 3.4 %copy-start.6 = (f32[8,10,512]{2,0,1:T(8,128)S(1)}, f32[8,10,512]{2,0,1:T(8,128)}, u32[]{:S(2)}) copy-start(f32[8,10,512]{2,0,1:T(8,128)} %get-tuple-element.260) | copy-start | bytes 491524 | tf_op jit(solution)/shard_map/while
  214.0 3.4 %copy-start.7 = (f32[8,10,512]{2,0,1:T(8,128)S(1)}, f32[8,10,512]{2,0,1:T(8,128)}, u32[]{:S(2)}) copy-start(f32[8,10,512]{2,0,1:T(8,128)} %get-tuple-element.249) | copy-start | bytes 491524 | tf_op jit(solution)/shard_map/while
  214.1 3.4 %copy-start.8 = (f32[8,10,512]{2,0,1:T(8,128)S(1)}, f32[8,10,512]{2,0,1:T(8,128)}, u32[]{:S(2)}) copy-start(f32[8,10,512]{2,0,1:T(8,128)} %get-tuple-element.258) | copy-start | bytes 491524 | tf_op jit(solution)/shard_map/while
  214.1 3.4 %copy-start.9 = (f32[8,10,512]{2,0,1:T(8,128)S(1)}, f32[8,10,512]{2,0,1:T(8,128)}, u32[]{:S(2)}) copy-start(f32[8,10,512]{2,0,1:T(8,128)} %get-tuple-element.247) | copy-start | bytes 491524 | tf_op jit(solution)/shard_map/while
  214.1 3.4 %copy-start.10 = (f32[8,10,512]{2,0,1:T(8,128)S(1)}, f32[8,10,512]{2,0,1:T(8,128)}, u32[]{:S(2)}) copy-start(f32[8,10,512]{2,0,1:T(8,128)} %get-tuple-element.256) | copy-start | bytes 491524 | tf_op jit(solution)/shard_map/while
  214.1 3.4 %copy-start.11 = (f32[8,10,512]{2,0,1:T(8,128)S(1)}, f32[8,10,512]{2,0,1:T(8,128)}, u32[]{:S(2)}) copy-start(f32[8,10,512]{2,0,1:T(8,128)} %get-tuple-element.245) | copy-start | bytes 491524 | tf_op jit(solution)/shard_map/while
  214.1 3.4 %copy-start.12 = (f32[8,10,512]{2,0,1:T(8,128)S(1)}, f32[8,10,512]{2,0,1:T(8,128)}, u32[]{:S(2)}) copy-start(f32[8,10,512]{2,0,1:T(8,128)} %get-tuple-element.254) | copy-start | bytes 491524 | tf_op jit(solution)/shard_map/while
  214.1 3.4 %copy-start.13 = (f32[8,10,512]{2,0,1:T(8,128)S(1)}, f32[8,10,512]{2,0,1:T(8,128)}, u32[]{:S(2)}) copy-start(f32[8,10,512]{2,0,1:T(8,128)} %get-tuple-element.243) | copy-start | bytes 491524 | tf_op jit(solution)/shard_map/while
  214.1 3.4 %copy-start.22 = (f32[1,512]{1,0:T(1,128)S(1)}, f32[1,512]{1,0:T(1,128)}, u32[]{:S(2)}) copy-start(f32[1,512]{1,0:T(1,128)} %get-tuple-element.257) | copy-start | bytes 6148 | tf_op jit(solution)/shard_map/while
  214.1 3.4 %copy-start.23 = (f32[1,512]{1,0:T(1,128)S(1)}, f32[1,512]{1,0:T(1,128)}, u32[]{:S(2)}) copy-start(f32[1,512]{1,0:T(1,128)} %get-tuple-element.259) | copy-start | bytes 6148 | tf_op jit(solution)/shard_map/while
  214.1 3.4 %copy-start.24 = (bf16[2,8,5,512]{3,1,2,0:T(8,128)(2,1)S(1)}, bf16[2,8,5,512]{3,1,2,0:T(8,128)(2,1)}, u32[]{:S(2)}) copy-start(bf16[2,8,5,512]{3,1,2,0:T(8,128)(2,1)} %get-tuple-element.272) | copy-start | bytes 245764 | tf_op jit(solution)/shard_map/while
  (26 other events, 71.9 us)
where the time goes:
time: 232 us; the launch traced here: 230 us
  local copies, waits for them, and re-layouts  154 us (66%)
  other arithmetic  35.5 us (15%)
  blocking collectives  20.3 us (9%)
  starting transfers between devices  10.6 us (5%)
  waiting for transfers between devices  6.83 us (3%)
    gather x48, local copies, waits for them, and re-layouts, face_flux(): taken = jnp.take(stacked, neighbors[face_index], axis=2)  133 us
    select_n x24, other arithmetic, face_flux(): taken = jnp.take(stacked, neighbors[face_index], axis=2)  15.6 us
    psum x1, blocking collectives, local(): return lax.psum(closure_part, 'cell')  10.7 us
    ppermute x4, starting transfers between devices, from_behind(): return lax.ppermute(shard, axis, pairs)  10.6 us
    all_gather x1, blocking collectives, local(): whole_basis = lax.all_gather(basis, ('snap', 'var'), axis=0, tiled=True)  9.68 us
    concatenate x4, local copies, waits for them, and re-layouts, face_flux(): stacked = jnp.concatenate([extended, product], axis=1)  8.67 us
    ppermute x4, waiting for transfers between devices, from_behind(): return lax.ppermute(shard, axis, pairs)  6.83 us
    and x12, other arithmetic, face_flux(): taken = jnp.take(stacked, neighbors[face_index], axis=2)  6.67 us
  transfers between devices with their start and end apart: 4, of which 3 were waited for; matrix products, arithmetic and copies ran while one was open for 1% of the time, Pallas kernels for 0%

commit v1 on v0

--- a/solution.py
+++ b/solution.py
@@ -39,7 +39,20 @@
         return (jnp.take(field, send_lists[0], axis=2), jnp.take(field, send_lists[1], axis=2))
 
     true_to_prev, true_to_next = rim_rows(q_true)
-    whole_basis = lax.all_gather(basis, ("snap", "var"), axis=0, tiled=True)
+    value = basis
+    ways, here, step = (
+        lax.axis_size(("snap", "var")),
+        lax.axis_index(("snap", "var")),
+        value.shape[0],
+    )
+    lengths = [n * ways if d == 0 else n for d, n in enumerate(value.shape)]
+    full = lax.dynamic_update_slice_in_dim(
+        jnp.zeros(lengths, value.dtype), value, here * step, axis=0
+    )
+    for far in range(1, ways):
+        value = lax.ppermute(value, ("snap", "var"), [(d, (d + 1) % ways) for d in range(ways)])
+        full = lax.dynamic_update_slice_in_dim(full, value, (here - far) % ways * step, axis=0)
+    whole_basis = full
     basis_flat = whole_basis.reshape(whole_basis.shape[0], var_count * cell_count)
     rebuilt_sum = jnp.dot(coeffs, basis_flat, preferred_element_type=jnp.float32)
     rebuilt = rebuilt_sum.astype(jnp.bfloat16).reshape(snap_count, var_count, cell_count)

time: 232 us -> 253 us (1.091)
  local copies, waits for them, and re-layouts: 154 us -> 172 us
  waiting for transfers between devices: 6.83 us -> 17.4 us
  blocking collectives: 20.3 us -> 10.6 us
    dynamic_update_slice x0 -> x4, local copies, waits for them, and re-layouts: none -> 14.6 us  [the longest x3 12.5 us: local(): lax.dynamic_update_slice_in_dim(full, value, (here - far) % ways * step,...]
    all_gather x1 -> x0, blocking collectives: 9.68 us -> none  [local(): whole_basis = lax.all_gather(basis, ('snap', 'var'), axis=0, tiled=True)]
    ppermute x0 -> x3, waiting for transfers between devices: none -> 9.08 us  [local(): lax.ppermute(value, ('snap', 'var'), [(d, (d + 1) % ways) for d in range(...]
  transfers between devices with their start and end apart: 4 -> 7, of which waited for: 3 -> 5; matrix products, arithmetic and copies ran while one was open for 1% -> 7% of each run, Pallas kernels for 0% -> 0%
where the time goes in v1:
time: 253 us; the launch traced here: 251 us
  local copies, waits for them, and re-layouts  172 us (68%)
  other arithmetic  36.2 us (14%)
  waiting for transfers between devices  17.4 us (7%)
  starting transfers between devices  12 us (5%)
  blocking collectives  10.6 us (4%)
    gather x48, local copies, waits for them, and re-layouts, face_flux(): taken = jnp.take(stacked, neighbors[face_index], axis=2)  134 us
    select_n x24, other arithmetic, face_flux(): taken = jnp.take(stacked, neighbors[face_index], axis=2)  15.4 us
    dynamic_update_slice x3, local copies, waits for them, and re-layouts, local(): lax.dynamic_update_slice_in_dim(full, value, (here - far) % ways * step,...  12.5 us
    ppermute x4, starting transfers between devices, from_behind(): return lax.ppermute(shard, axis, pairs)  11.5 us
    psum x1, blocking collectives, local(): return lax.psum(closure_part, 'cell')  10.6 us
    ppermute x3, waiting for transfers between devices, local(): lax.ppermute(value, ('snap', 'var'), [(d, (d + 1) % ways) for d in range(...  9.08 us
    concatenate x4, local copies, waits for them, and re-layouts, face_flux(): stacked = jnp.concatenate([extended, product], axis=1)  8.67 us
    ppermute x4, waiting for transfers between devices, from_behind(): return lax.ppermute(shard, axis, pairs)  8.36 us
  transfers between devices with their start and end apart: 7, of which 5 were waited for; matrix products, arithmetic and copies ran while one was open for 7% of the time, Pallas kernels for 0%

profile of v1, /device:TPU:0, one launch (start us, length us, event | category | flops | bytes accessed | tf_op | source)
XLA Modules:
  0.0 251.1 jit_solution(8334772980485077125)
XLA Ops:
  0.5 5.1 %collective-permute-done.2 = bf16[32,5,512]{2,0,1:T(8,128)(2,1)S(1)} collective-permute-done((bf16[32,5,512]{2,0,1:T(8,128)(2,1)}, bf16[32,5,512]{2,0,1:T(8,128)(2,1)S(1)}, u32[]{:S(2)}, u32[]{:S(2)}) %collective-permute-start.2) | collective-permute-done | bytes 163872 | tf_op jit(solution)/shard_map/ppermute | solution.py:53
  6.4 3.9 %collective-permute-done.3 = bf16[32,5,512]{2,0,1:T(8,128)(2,1)S(1)} collective-permute-done((bf16[32,5,512]{2,0,1:T(8,128)(2,1)S(1)}, bf16[32,5,512]{2,0,1:T(8,128)(2,1)S(1)}, u32[]{:S(2)}, u32[]{:S(2)}) %collective-permute-start.3) | collective-permute-done | bytes 163872 | tf_op jit(solution)/shard_map/ppermute | solution.py:53
  17.3 4.2 %dynamic_update_slice.17 = bf16[128,5,512]{0,2,1:T(8,128)(2,1)S(1)} dynamic-update-slice(bf16[128,5,512]{0,2,1:T(8,128)(2,1)S(1)} %dynamic_update_slice.16, bf16[32,5,512]{0,2,1:T(8,128)(2,1)S(1)} %copy.133, s32[]{:T(128)S(6)} %select_n.43, s32[]{:T(128)} %copy.189, s32[]{:T(128)} %copy.189) | dynamic-update-slice | bytes 327684 | tf_op jit(solution)/shard_map/dynamic_update_slice | solution.py:54
  21.8 4.2 %dynamic_update_slice.18 = bf16[128,5,512]{0,2,1:T(8,128)(2,1)S(1)} dynamic-update-slice(bf16[128,5,512]{0,2,1:T(8,128)(2,1)S(1)} %dynamic_update_slice.17, bf16[32,5,512]{0,2,1:T(8,128)(2,1)S(1)} %copy.134, s32[]{:T(128)S(6)} %select_n.45, s32[]{:T(128)} %copy.189, s32[]{:T(128)} %copy.189) | dynamic-update-slice | bytes 327684 | tf_op jit(solution)/shard_map/dynamic_update_slice | solution.py:54
  26.3 4.2 %dynamic_update_slice.19 = bf16[128,5,512]{0,2,1:T(8,128)(2,1)S(1)} dynamic-update-slice(bf16[128,5,512]{0,2,1:T(8,128)(2,1)S(1)} %dynamic_update_slice.18, bf16[32,5,512]{0,2,1:T(8,128)(2,1)S(1)} %copy.135, s32[]{:T(128)S(6)} %select_n.47, s32[]{:T(128)} %copy.189, s32[]{:T(128)} %copy.189) | dynamic-update-slice | bytes 327684 | tf_op jit(solution)/shard_map/dynamic_update_slice | solution.py:54
  33.3 4.3 %collective-permute-start = (bf16[16,5,128]{0,1,2:T(8,128)(2,1)S(1)}, bf16[16,5,128]{0,1,2:T(8,128)(2,1)S(1)}, u32[]{:S(2)}, u32[]{:S(2)}) collective-permute-start(bf16[16,5,128]{0,1,2:T(8,128)(2,1)S(1)} %get-tuple-element.158), channel_id=1, source_target_pairs={{0,4},{4,8},{8,12},{1,5},{5,9},{9,13},{2,6},{6,10},{10,14},{3,7},{... | collective-permute-start | bytes 61448 | tf_op jit(solution)/shard_map/ppermute | solution.py:13
  39.8 4.6 %collective-permute-start.5 = (bf16[16,5,128]{0,1,2:T(8,128)(2,1)S(1)}, bf16[16,5,128]{0,1,2:T(8,128)(2,1)S(1)}, u32[]{:S(2)}, u32[]{:S(2)}) collective-permute-start(bf16[16,5,128]{0,1,2:T(8,128)(2,1)S(1)} %get-tuple-element.157), channel_id=1, source_target_pairs={{0,4},{4,8},{8,12},{1,5},{5,9},{9,13},{2,6},{6,10},{10,14},{3,7},{... | collective-permute-start | bytes 61448 | tf_op jit(solution)/shard_map/ppermute | solution.py:13
  51.2 4.0 %collective-permute-done.6 = bf16[16,5,128]{0,1,2:T(8,128)(2,1)S(1)} collective-permute-done((bf16[16,5,128]{0,1,2:T(8,128)(2,1)S(1)}, bf16[16,5,128]{0,1,2:T(8,128)(2,1)S(1)}, u32[]{:S(2)}, u32[]{:S(2)}) %collective-permute-start.6) | collective-permute-done | bytes 20512 | tf_op jit(solution)/shard_map/ppermute | solution.py:13
  56.0 183.2 %while.11 = (s32[]{:T(128)}, bf16[2,8,5,512]{3,1,2,0:T(8,128)(2,1)}, f32[5,512]{1,0:T(8,128)}, f32[6,512]{1,0:T(8,128)}, bf16[2,8,5,768]{3,1,0,2:T(8,128)(2,1)},...) while((s32[]{:T(128)}, bf16[2,8,5,512]{3,1,2,0:T(8,128)(2,1)}, ...), condition=%wide.region_1.4_spmd.clone, body=%wide.region_0.3_spmd.clone.sunk | while | flops 2576898 | bytes 26092312 | solution.py:79
  72.4 2.9 %copy.175 = f32[512,8,10]{0,1,2:T(8,128)} copy(f32[512,8,10]{2,1,0:T(8,128)} %gather_fusion.11) | data formatting | bytes 327680 | tf_op jit(solution)/shard_map/while/body/eval_jaxpr/jit(_take)/gather | solution.py:25
  78.0 2.9 %copy.173 = f32[512,8,10]{0,1,2:T(8,128)} copy(f32[512,8,10]{2,1,0:T(8,128)} %gather_fusion.9) | data formatting | bytes 327680 | tf_op jit(solution)/shard_map/while/body/eval_jaxpr/jit(_take)/gather | solution.py:25
  83.6 2.9 %copy.171 = f32[512,8,10]{0,1,2:T(8,128)} copy(f32[512,8,10]{2,1,0:T(8,128)} %gather_fusion.7) | data formatting | bytes 327680 | tf_op jit(solution)/shard_map/while/body/eval_jaxpr/jit(_take)/gather | solution.py:25
  89.1 2.9 %copy.169 = f32[512,8,10]{0,1,2:T(8,128)} copy(f32[512,8,10]{2,1,0:T(8,128)} %gather_fusion.5) | data formatting | bytes 327680 | tf_op jit(solution)/shard_map/while/body/eval_jaxpr/jit(_take)/gather | solution.py:25
  94.7 2.9 %copy.167 = f32[512,8,10]{0,1,2:T(8,128)} copy(f32[512,8,10]{2,1,0:T(8,128)} %gather_fusion.3) | data formatting | bytes 327680 | tf_op jit(solution)/shard_map/while/body/eval_jaxpr/jit(_take)/gather | solution.py:25
  100.3 2.9 %copy.165 = f32[512,8,10]{0,1,2:T(8,128)} copy(f32[512,8,10]{2,1,0:T(8,128)} %gather_fusion.1) | data formatting | bytes 327680 | tf_op jit(solution)/shard_map/while/body/eval_jaxpr/jit(_take)/gather | solution.py:25
  108.2 2.9 %copy.174 = f32[512,8,10]{0,1,2:T(8,128)} copy(f32[512,8,10]{2,1,0:T(8,128)} %gather_fusion.10) | data formatting | bytes 327680 | tf_op jit(solution)/shard_map/while/body/eval_jaxpr/jit(_take)/gather | solution.py:25
  115.5 2.9 %copy.172 = f32[512,8,10]{0,1,2:T(8,128)} copy(f32[512,8,10]{2,1,0:T(8,128)} %gather_fusion.8) | data formatting | bytes 327680 | tf_op jit(solution)/shard_map/while/body/eval_jaxpr/jit(_take)/gather | solution.py:25
  122.8 2.9 %copy.170 = f32[512,8,10]{0,1,2:T(8,128)} copy(f32[512,8,10]{2,1,0:T(8,128)} %gather_fusion.6) | data formatting | bytes 327680 | tf_op jit(solution)/shard_map/while/body/eval_jaxpr/jit(_take)/gather | solution.py:25
  130.2 2.9 %copy.168 = f32[512,8,10]{0,1,2:T(8,128)} copy(f32[512,8,10]{2,1,0:T(8,128)} %gather_fusion.4) | data formatting | bytes 327680 | tf_op jit(solution)/shard_map/while/body/eval_jaxpr/jit(_take)/gather | solution.py:25
  137.6 2.9 %copy.166 = f32[512,8,10]{0,1,2:T(8,128)} copy(f32[512,8,10]{2,1,0:T(8,128)} %gather_fusion.2) | data formatting | bytes 327680 | tf_op jit(solution)/shard_map/while/body/eval_jaxpr/jit(_take)/gather | solution.py:25
  164.0 2.9 %copy.175 = f32[512,8,10]{0,1,2:T(8,128)} copy(f32[512,8,10]{2,1,0:T(8,128)} %gather_fusion.11) | data formatting | bytes 327680 | tf_op jit(solution)/shard_map/while/body/eval_jaxpr/jit(_take)/gather | solution.py:25
  169.6 2.9 %copy.173 = f32[512,8,10]{0,1,2:T(8,128)} copy(f32[512,8,10]{2,1,0:T(8,128)} %gather_fusion.9) | data formatting | bytes 327680 | tf_op jit(solution)/shard_map/while/body/eval_jaxpr/jit(_take)/gather | solution.py:25
  175.1 2.9 %copy.171 = f32[512,8,10]{0,1,2:T(8,128)} copy(f32[512,8,10]{2,1,0:T(8,128)} %gather_fusion.7) | data formatting | bytes 327680 | tf_op jit(solution)/shard_map/while/body/eval_jaxpr/jit(_take)/gather | solution.py:25
  180.7 2.9 %copy.169 = f32[512,8,10]{0,1,2:T(8,128)} copy(f32[512,8,10]{2,1,0:T(8,128)} %gather_fusion.5) | data formatting | bytes 327680 | tf_op jit(solution)/shard_map/while/body/eval_jaxpr/jit(_take)/gather | solution.py:25
  186.3 2.9 %copy.167 = f32[512,8,10]{0,1,2:T(8,128)} copy(f32[512,8,10]{2,1,0:T(8,128)} %gather_fusion.3) | data formatting | bytes 327680 | tf_op jit(solution)/shard_map/while/body/eval_jaxpr/jit(_take)/gather | solution.py:25
  191.9 2.9 %copy.165 = f32[512,8,10]{0,1,2:T(8,128)} copy(f32[512,8,10]{2,1,0:T(8,128)} %gather_fusion.1) | data formatting | bytes 327680 | tf_op jit(solution)/shard_map/while/body/eval_jaxpr/jit(_take)/gather | solution.py:25
  199.7 2.9 %copy.174 = f32[512,8,10]{0,1,2:T(8,128)} copy(f32[512,8,10]{2,1,0:T(8,128)} %gather_fusion.10) | data formatting | bytes 327680 | tf_op jit(solution)/shard_map/while/body/eval_jaxpr/jit(_take)/gather | solution.py:25
  207.1 2.9 %copy.172 = f32[512,8,10]{0,1,2:T(8,128)} copy(f32[512,8,10]{2,1,0:T(8,128)} %gather_fusion.8) | data formatting | bytes 327680 | tf_op jit(solution)/shard_map/while/body/eval_jaxpr/jit(_take)/gather | solution.py:25
  214.4 2.9 %copy.170 = f32[512,8,10]{0,1,2:T(8,128)} copy(f32[512,8,10]{2,1,0:T(8,128)} %gather_fusion.6) | data formatting | bytes 327680 | tf_op jit(solution)/shard_map/while/body/eval_jaxpr/jit(_take)/gather | solution.py:25
  221.8 2.9 %copy.168 = f32[512,8,10]{0,1,2:T(8,128)} copy(f32[512,8,10]{2,1,0:T(8,128)} %gather_fusion.4) | data formatting | bytes 327680 | tf_op jit(solution)/shard_map/while/body/eval_jaxpr/jit(_take)/gather | solution.py:25
  229.2 2.9 %copy.166 = f32[512,8,10]{0,1,2:T(8,128)} copy(f32[512,8,10]{2,1,0:T(8,128)} %gather_fusion.2) | data formatting | bytes 327680 | tf_op jit(solution)/shard_map/while/body/eval_jaxpr/jit(_take)/gather | solution.py:25
  240.4 10.6 %psum.7 = f32[16,128]{1,0:T(8,128)} all-reduce(f32[16,128]{1,0:T(8,128)S(1)} %fusion.66), channel_id=1, replica_groups=mesh['grp'=2,'cell'=4,'snap'=2,'var'=2] {'cell'}, use_global_device_ids=true, to_apply=%region_2.5 | all-reduce | flops 2048 | bytes 16384 | tf_op jit(solution)/shard_map/psum | solution.py:85
  (240 shorter events, 140.8 us)
Async XLA Ops:
  0.0 30.5 %copy-start = (bf16[16,128]{1,0:T(8,128)(2,1)S(1)}, bf16[16,128]{1,0:T(8,128)(2,1)}, u32[]{:S(2)}) copy-start(bf16[16,128]{1,0:T(8,128)(2,1)} %param.15) | copy-start | bytes 12292
  0.0 5.6 %collective-permute-start.2 = (bf16[32,5,512]{2,0,1:T(8,128)(2,1)}, bf16[32,5,512]{2,0,1:T(8,128)(2,1)S(1)}, u32[]{:S(2)}, u32[]{:S(2)}) collective-permute-start(bf16[32,5,512]{2,0,1:T(8,128)(2,1)} %param.16), channel_id=1, source_target_pairs={{0,1},{1,2},{2,3},{3,0},{4,5},{5,6},{6,7},{7,4},{8,9},{9,10},{10,1... | collective-permute-start | bytes 491528 | tf_op jit(solution)/shard_map/ppermute | solution.py:53
  5.6 4.7 %collective-permute-start.3 = (bf16[32,5,512]{2,0,1:T(8,128)(2,1)S(1)}, bf16[32,5,512]{2,0,1:T(8,128)(2,1)S(1)}, u32[]{:S(2)}, u32[]{:S(2)}) collective-permute-start(bf16[32,5,512]{2,0,1:T(8,128)(2,1)S(1)} %collective-permute-done.2), channel_id=1, source_target_pairs={{0,1},{1,2},{2,3},{3,0},{4,5},{5,6},{6,7},{7,4},{8,9},{9,10},{10,1... | collective-permute-start | bytes 491528 | tf_op jit(solution)/shard_map/ppermute | solution.py:53
  10.3 15.6 %collective-permute-start.4 = (bf16[32,5,512]{2,0,1:T(8,128)(2,1)S(1)}, bf16[32,5,512]{2,0,1:T(8,128)(2,1)S(1)}, u32[]{:S(2)}, u32[]{:S(2)}) collective-permute-start(bf16[32,5,512]{2,0,1:T(8,128)(2,1)S(1)} %collective-permute-done.3), channel_id=1, source_target_pairs={{0,1},{1,2},{2,3},{3,0},{4,5},{5,6},{6,7},{7,4},{8,9},{9,10},{10,1... | collective-permute-start | bytes 491528 | tf_op jit(solution)/shard_map/ppermute | solution.py:53
  30.5 7.4 %copy-start.14 = (bf16[128,5,512]{0,2,1:T(8,128)(2,1)}, bf16[128,5,512]{0,2,1:T(8,128)(2,1)S(1)}, u32[]{:S(2)}) copy-start(bf16[128,5,512]{0,2,1:T(8,128)(2,1)S(1)} %dynamic_update_slice.19) | copy-start | bytes 1966084
  30.7 18.0 %copy-start.15 = (bf16[16,5,512]{2,0,1:T(8,128)(2,1)S(1)}, bf16[16,5,512]{2,0,1:T(8,128)(2,1)}, u32[]{:S(2)}) copy-start(bf16[16,5,512]{2,0,1:T(8,128)(2,1)} %param.14) | copy-start | bytes 245764
  33.3 12.4 %collective-permute-start = (bf16[16,5,128]{0,1,2:T(8,128)(2,1)S(1)}, bf16[16,5,128]{0,1,2:T(8,128)(2,1)S(1)}, u32[]{:S(2)}, u32[]{:S(2)}) collective-permute-start(bf16[16,5,128]{0,1,2:T(8,128)(2,1)S(1)} %get-tuple-element.158), channel_id=1, source_target_pairs={{0,4},{4,8},{8,12},{1,5},{5,9},{9,13},{2,6},{6,10},{10,14},{3,7},{... | collective-permute-start | bytes 61448 | tf_op jit(solution)/shard_map/ppermute | solution.py:13
  37.8 10.8 %collective-permute-start.1 = (bf16[16,5,128]{0,1,2:T(8,128)(2,1)S(1)}, bf16[16,5,128]{0,1,2:T(8,128)(2,1)S(1)}, u32[]{:S(2)}, u32[]{:S(2)}) collective-permute-start(bf16[16,5,128]{0,1,2:T(8,128)(2,1)S(1)} %get-tuple-element.160), channel_id=1, source_target_pairs={{4,0},{8,4},{12,8},{5,1},{9,5},{13,9},{6,2},{10,6},{14,10},{7,3},{... | collective-permute-start | bytes 61448 | tf_op jit(solution)/shard_map/ppermute | solution.py:13
  39.8 11.2 %collective-permute-start.5 = (bf16[16,5,128]{0,1,2:T(8,128)(2,1)S(1)}, bf16[16,5,128]{0,1,2:T(8,128)(2,1)S(1)}, u32[]{:S(2)}, u32[]{:S(2)}) collective-permute-start(bf16[16,5,128]{0,1,2:T(8,128)(2,1)S(1)} %get-tuple-element.157), channel_id=1, source_target_pairs={{0,4},{4,8},{8,12},{1,5},{5,9},{9,13},{2,6},{6,10},{10,14},{3,7},{... | collective-permute-start | bytes 61448 | tf_op jit(solution)/shard_map/ppermute | solution.py:13
  44.3 10.8 %collective-permute-start.6 = (bf16[16,5,128]{0,1,2:T(8,128)(2,1)S(1)}, bf16[16,5,128]{0,1,2:T(8,128)(2,1)S(1)}, u32[]{:S(2)}, u32[]{:S(2)}) collective-permute-start(bf16[16,5,128]{0,1,2:T(8,128)(2,1)S(1)} %get-tuple-element.159), channel_id=1, source_target_pairs={{4,0},{8,4},{12,8},{5,1},{9,5},{13,9},{6,2},{10,6},{14,10},{7,3},{... | collective-permute-start | bytes 61448 | tf_op jit(solution)/shard_map/ppermute | solution.py:13
  118.4 7.4 %copy-start.26 = (pred[512]{0:T(512)(128)(4,1)S(1)}, pred[512]{0:T(512)(128)(4,1)}, u32[]{:S(2)}) copy-start(pred[512]{0:T(512)(128)(4,1)} %compare_and_fusion.17) | copy-start | bytes 1540 | tf_op jit(solution)/shard_map/while
  125.7 7.4 %copy-start.25 = (pred[512]{0:T(512)(128)(4,1)S(1)}, pred[512]{0:T(512)(128)(4,1)}, u32[]{:S(2)}) copy-start(pred[512]{0:T(512)(128)(4,1)} %compare_and_fusion.16) | copy-start | bytes 1540 | tf_op jit(solution)/shard_map/while
  140.5 6.0 %copy-start.16 = (f32[1,512]{1,0:T(1,128)S(1)}, f32[1,512]{1,0:T(1,128)}, u32[]{:S(2)}) copy-start(f32[1,512]{1,0:T(1,128)} %get-tuple-element.261) | copy-start | bytes 6148 | tf_op jit(solution)/shard_map/while
  140.5 6.0 %copy-start.17 = (f32[1,512]{1,0:T(1,128)S(1)}, f32[1,512]{1,0:T(1,128)}, u32[]{:S(2)}) copy-start(f32[1,512]{1,0:T(1,128)} %get-tuple-element.251) | copy-start | bytes 6148 | tf_op jit(solution)/shard_map/while
  140.5 6.0 %copy-start.18 = (f32[1,512]{1,0:T(1,128)S(1)}, f32[1,512]{1,0:T(1,128)}, u32[]{:S(2)}) copy-start(f32[1,512]{1,0:T(1,128)} %get-tuple-element.253) | copy-start | bytes 6148 | tf_op jit(solution)/shard_map/while
  140.5 6.0 %copy-start.19 = (f32[1,512]{1,0:T(1,128)S(1)}, f32[1,512]{1,0:T(1,128)}, u32[]{:S(2)}) copy-start(f32[1,512]{1,0:T(1,128)} %get-tuple-element.255) | copy-start | bytes 6148 | tf_op jit(solution)/shard_map/while
  209.9 7.4 %copy-start.26 = (pred[512]{0:T(512)(128)(4,1)S(1)}, pred[512]{0:T(512)(128)(4,1)}, u32[]{:S(2)}) copy-start(pred[512]{0:T(512)(128)(4,1)} %compare_and_fusion.17) | copy-start | bytes 1540 | tf_op jit(solution)/shard_map/while
  217.3 7.4 %copy-start.25 = (pred[512]{0:T(512)(128)(4,1)S(1)}, pred[512]{0:T(512)(128)(4,1)}, u32[]{:S(2)}) copy-start(pred[512]{0:T(512)(128)(4,1)} %compare_and_fusion.16) | copy-start | bytes 1540 | tf_op jit(solution)/shard_map/while
  232.0 6.0 %copy-start.16 = (f32[1,512]{1,0:T(1,128)S(1)}, f32[1,512]{1,0:T(1,128)}, u32[]{:S(2)}) copy-start(f32[1,512]{1,0:T(1,128)} %get-tuple-element.261) | copy-start | bytes 6148 | tf_op jit(solution)/shard_map/while
  232.0 6.0 %copy-start.17 = (f32[1,512]{1,0:T(1,128)S(1)}, f32[1,512]{1,0:T(1,128)}, u32[]{:S(2)}) copy-start(f32[1,512]{1,0:T(1,128)} %get-tuple-element.251) | copy-start | bytes 6148 | tf_op jit(solution)/shard_map/while
  232.0 6.0 %copy-start.18 = (f32[1,512]{1,0:T(1,128)S(1)}, f32[1,512]{1,0:T(1,128)}, u32[]{:S(2)}) copy-start(f32[1,512]{1,0:T(1,128)} %get-tuple-element.253) | copy-start | bytes 6148 | tf_op jit(solution)/shard_map/while
  232.1 6.0 %copy-start.19 = (f32[1,512]{1,0:T(1,128)S(1)}, f32[1,512]{1,0:T(1,128)}, u32[]{:S(2)}) copy-start(f32[1,512]{1,0:T(1,128)} %get-tuple-element.255) | copy-start | bytes 6148 | tf_op jit(solution)/shard_map/while
  234.8 3.3 %copy-start.2 = (f32[8,5,768]{2,0,1:T(8,128)S(1)}, f32[8,5,768]{2,0,1:T(8,128)}, u32[]{:S(2)}) copy-start(f32[8,5,768]{2,0,1:T(8,128)} %copy-done.1) | copy-start | bytes 368644 | tf_op jit(solution)/shard_map/while
  234.8 3.3 %copy-start.6 = (f32[8,10,512]{2,0,1:T(8,128)S(1)}, f32[8,10,512]{2,0,1:T(8,128)}, u32[]{:S(2)}) copy-start(f32[8,10,512]{2,0,1:T(8,128)} %get-tuple-element.260) | copy-start | bytes 491524 | tf_op jit(solution)/shard_map/while
  234.8 3.3 %copy-start.7 = (f32[8,10,512]{2,0,1:T(8,128)S(1)}, f32[8,10,512]{2,0,1:T(8,128)}, u32[]{:S(2)}) copy-start(f32[8,10,512]{2,0,1:T(8,128)} %get-tuple-element.249) | copy-start | bytes 491524 | tf_op jit(solution)/shard_map/while
  234.8 3.3 %copy-start.8 = (f32[8,10,512]{2,0,1:T(8,128)S(1)}, f32[8,10,512]{2,0,1:T(8,128)}, u32[]{:S(2)}) copy-start(f32[8,10,512]{2,0,1:T(8,128)} %get-tuple-element.258) | copy-start | bytes 491524 | tf_op jit(solution)/shard_map/while
  234.8 3.3 %copy-start.9 = (f32[8,10,512]{2,0,1:T(8,128)S(1)}, f32[8,10,512]{2,0,1:T(8,128)}, u32[]{:S(2)}) copy-start(f32[8,10,512]{2,0,1:T(8,128)} %get-tuple-element.247) | copy-start | bytes 491524 | tf_op jit(solution)/shard_map/while
  234.8 3.3 %copy-start.10 = (f32[8,10,512]{2,0,1:T(8,128)S(1)}, f32[8,10,512]{2,0,1:T(8,128)}, u32[]{:S(2)}) copy-start(f32[8,10,512]{2,0,1:T(8,128)} %get-tuple-element.256) | copy-start | bytes 491524 | tf_op jit(solution)/shard_map/while
  234.8 3.3 %copy-start.11 = (f32[8,10,512]{2,0,1:T(8,128)S(1)}, f32[8,10,512]{2,0,1:T(8,128)}, u32[]{:S(2)}) copy-start(f32[8,10,512]{2,0,1:T(8,128)} %get-tuple-element.245) | copy-start | bytes 491524 | tf_op jit(solution)/shard_map/while
  234.8 3.3 %copy-start.12 = (f32[8,10,512]{2,0,1:T(8,128)S(1)}, f32[8,10,512]{2,0,1:T(8,128)}, u32[]{:S(2)}) copy-start(f32[8,10,512]{2,0,1:T(8,128)} %get-tuple-element.254) | copy-start | bytes 491524 | tf_op jit(solution)/shard_map/while
  234.9 3.3 %copy-start.13 = (f32[8,10,512]{2,0,1:T(8,128)S(1)}, f32[8,10,512]{2,0,1:T(8,128)}, u32[]{:S(2)}) copy-start(f32[8,10,512]{2,0,1:T(8,128)} %get-tuple-element.243) | copy-start | bytes 491524 | tf_op jit(solution)/shard_map/while
  234.9 3.3 %copy-start.20 = (f32[1,512]{1,0:T(1,128)S(1)}, f32[1,512]{1,0:T(1,128)}, u32[]{:S(2)}) copy-start(f32[1,512]{1,0:T(1,128)} %get-tuple-element.257) | copy-start | bytes 6148 | tf_op jit(solution)/shard_map/while
  (26 other events, 72.9 us)
